TPU v7x, 32 devices: a whole 2x2x4 slice. The times are simulated.
32 devices in a mesh: dp: 16 (over z, y, x), mp: 2 (over core).
Axes of the slice: x: 2, y: 2, z: 4, core: 2. Of those that a mesh axis runs over, the one named last changes fastest.
Arguments:
- value_grads: bfloat16 [16, 24, 128, 128], P('dp', 'mp'), may hold values from -2 to 2
- key_grads: bfloat16 [16, 2, 16, 128, 128], P('dp', 'mp'), may hold values from -0.75 to 0.75
- owners: int32 [40, 1], P('mp'), may hold values from 0 to 15; in each aligned block of 20 rows (0 to 19, 20 to 39, ...) at most 2 rows name the same one
- weights: float32 [16, 2, 2, 128, 128], P('dp', 'mp'), may hold values from -6 to 6
- left: float32 [16, 2, 2, 128, 128], P('dp', 'mp'), may hold values from -0.25 to 4, as said below
- right: float32 [16, 2, 2, 128, 128], P('dp', 'mp'), may hold values from -0.25 to 4, as said below
- left_root: float32 [16, 2, 2, 128, 128], P('dp', 'mp'), may hold values from -0.25 to 4
- right_root: float32 [16, 2, 2, 128, 128], P('dp', 'mp'), may hold values from -0.25 to 4
- second: float32 [16, 2, 2, 128, 128], P('dp', 'mp'), may hold values from 0.001 to 0.1
Outputs:
- new_weights: float32 [16, 2, 2, 128, 128], P('dp', 'mp')
- new_left: float32 [16, 2, 2, 128, 128], P('dp', 'mp')
- new_right: float32 [16, 2, 2, 128, 128], P('dp', 'mp')
- new_second: float32 [16, 2, 2, 128, 128], P('dp', 'mp')
- new_values: bfloat16 [24, 128, 128], P('mp')
- new_keys: bfloat16 [16, 128, 128], P('mp')
Inputs may be any that keep to these rules, and one draw needn't show every extreme that they name: `owners`: within each aligned block of 20 rows (one index of mp) no dp index appears more than 2 times; some appears exactly 2 times. `left`: Symmetric. `right`: Symmetric.
All inputs are finite; a program needn't handle non-finite values.
Results may differ from a plain program's by a relative error of at most 0.0035.
Values may be sent and summed in bfloat16 or wider, within the bound.
A program may use at most 64 MiB of HBM per device.

v0:
```python
import jax
import jax.numpy as jnp
from jax import lax
from jax.sharding import PartitionSpec as P

STAT_DECAY = 0.95
ADAM_DECAY = 0.95
LEARN_RATE = 0.1
NORM_EPS = 1e-06


def slot_onehot(owner_ids, capacity, slot_count):
    position = jnp.arange(owner_ids.shape[0], dtype=jnp.int32)
    same_owner = owner_ids[:, None] == owner_ids[None, :]
    earlier = position[None, :] < position[:, None]
    slot_rank = jnp.sum((same_owner & earlier).astype(jnp.int32), axis=1)
    target = owner_ids * capacity + slot_rank
    return (target[:, None] == jnp.arange(slot_count, dtype=jnp.int32)[None, :]).astype(
        jnp.bfloat16
    )


def shampoo(gradient, weights, left, right, left_root, right_root, second):
    high = lax.Precision.HIGHEST
    new_left = STAT_DECAY * left + (1.0 - STAT_DECAY) * jnp.einsum(
        "...ij,...kj->...ik", gradient, gradient, precision=high
    )
    new_right = STAT_DECAY * right + (1.0 - STAT_DECAY) * jnp.einsum(
        "...ji,...jk->...ik", gradient, gradient, precision=high
    )
    shaped = jnp.einsum("...ij,...jk->...ik", left_root, gradient, precision=high)
    shaped = jnp.einsum("...ij,...jk->...ik", shaped, right_root, precision=high)
    new_second = ADAM_DECAY * second + (1.0 - ADAM_DECAY) * gradient * gradient
    adam_step = gradient / jnp.sqrt(new_second)
    adam_norm = jnp.sqrt(jnp.sum(adam_step * adam_step, axis=(-2, -1), keepdims=True))
    shaped_norm = jnp.sqrt(jnp.sum(shaped * shaped, axis=(-2, -1), keepdims=True))
    graft_scale = adam_norm / (shaped_norm + NORM_EPS)
    new_weights = weights - LEARN_RATE * graft_scale * shaped
    return (new_weights, new_left, new_right, new_second)


def on_device(value_grads, key_grads, owners, weights, left, right, left_root, right_root, second):
    dp_count = lax.axis_size("dp")
    capacity = weights.shape[2]
    slot_count = dp_count * capacity
    value_count = value_grads.shape[1]
    side = value_grads.shape[2]
    key_part = lax.psum_scatter(
        key_grads.astype(jnp.float32).astype(jnp.bfloat16), "mp", scatter_dimension=2, tiled=True
    ).astype(jnp.float32)
    key_rows = key_part[0, 0].astype(jnp.bfloat16)
    one_hot = slot_onehot(owners[:, 0], capacity, slot_count)
    blocks = jnp.concatenate([value_grads[0], key_rows], axis=0)
    placed = jnp.einsum("bj,bxy->jxy", one_hot, blocks, preferred_element_type=jnp.float32)
    outgoing = placed.astype(jnp.bfloat16).reshape(dp_count, capacity, side, side)
    incoming = lax.all_to_all(outgoing, "dp", split_axis=0, concat_axis=0, tiled=True)
    gradient = jnp.sum(incoming, axis=0, dtype=jnp.float32)
    new_weights, new_left, new_right, new_second = shampoo(
        gradient,
        weights[0, 0],
        left[0, 0],
        right[0, 0],
        left_root[0, 0],
        right_root[0, 0],
        second[0, 0],
    )
    rounded = new_weights.astype(jnp.bfloat16)
    everyone = lax.all_gather(rounded, "dp", axis=0, tiled=True)
    picked = jnp.einsum(
        "bj,jxy->bxy", one_hot, everyone, preferred_element_type=jnp.float32
    ).astype(jnp.bfloat16)
    return (
        new_weights[None, None],
        new_left[None, None],
        new_right[None, None],
        new_second[None, None],
        picked[:value_count],
        picked[value_count:],
    )


def solution(mesh):
    return jax.shard_map(
        on_device,
        mesh=mesh,
        in_specs=(
            P("dp", "mp", None, None),
            P("dp", "mp", None, None, None),
            P("mp", None),
            P("dp", "mp", None, None, None),
            P("dp", "mp", None, None, None),
            P("dp", "mp", None, None, None),
            P("dp", "mp", None, None, None),
            P("dp", "mp", None, None, None),
            P("dp", "mp", None, None, None),
        ),
        out_specs=(
            P("dp", "mp", None, None, None),
            P("dp", "mp", None, None, None),
            P("dp", "mp", None, None, None),
            P("dp", "mp", None, None, None),
            P("mp", None, None),
            P("mp", None, None),
        ),
        check_vma=False,
    )
```

profile of v0, /device:TPU:0, one launch (start us, length us, event | category | flops | bytes accessed | tf_op | source)
XLA Modules:
  0.0 123.6 jit_solution(12774246260677728813)
XLA Ops:
  7.2 0.0 copy-start
  7.2 0.0 copy-start.2
  7.2 0.0 reduce-scatter.4.cloned.1.call-start
  7.2 0.0 copy-start.7
  7.2 2.2 %copy.86 = bf16[2,8,128,128]{3,1,2,0:T(8,128)(2,1)} copy(bf16[2,8,128,128]{3,2,1,0:T(8,128)(2,1)} %bitcast.74) | data formatting | bytes 1048576
  9.5 0.0 reduce-scatter.4.cloned.1.call-update
  9.5 0.0 all-gather.2.cloned.1.call-start
  9.5 0.0 copy-done.2
  9.6 0.3 copy.87
  9.8 0.0 copy-done.7
  9.8 0.2 convert_reduce_fusion.1
  10.0 10.9 %reduce-scatter.4.cloned.1.call-done = bf16[8,16384]{1,0:T(8,128)(2,1)} async-done(((bf16[16,16384]{1,0:T(8,128)(2,1)}), bf16[8,16384]{1,0:T(8,128)(2,1)}) %reduce-scatter.4.cloned.1.call-update) | async-done | bytes 262160
  20.9 1.0 copy.88
  21.9 0.2 copy.89
  22.1 0.6 convolution_convert_fusion
  22.7 1.0 copy.55
  23.6 33.3 %all_to_all.5 = bf16[16,2,128,128]{3,1,2,0:T(2,128)(2,1)S(1)} all-to-all(bf16[16,2,128,128]{3,1,2,0:T(2,128)(2,1)S(1)} %copy.55), channel_id=1, replica_groups=mesh['dp'=16,'mp'=2] {'dp'}, dimensions={0} | all-to-all | bytes 2097152 | tf_op jit(solution)/shard_map/all_to_all | solution.py:56
  56.9 0.0 copy-start.3
  56.9 0.0 copy-start.1
  56.9 0.0 copy-start.4
  56.9 0.1 convert_reduce_fusion
  57.0 0.8 copy-done.3
  57.8 0.0 copy-start.5
  57.8 0.0 copy-start.6
  57.8 0.3 fusion.16
  58.1 0.0 copy-done.1
  58.1 0.1 fusion.12
  58.2 0.0 copy-done
  58.2 0.4 multiply_reduce_fusion
  58.6 0.0 copy-done.4
  58.6 0.8 fusion.18
  59.4 0.0 all-gather.2.cloned.1.call-update
  59.4 0.0 copy-done.5
  59.4 1.0 fusion.1
  60.4 0.0 copy-done.6
  60.5 1.0 fusion.3
  61.5 0.7 fusion.13
  62.2 50.9 %all-gather.2.cloned.1.call-done = bf16[32,128,128]{2,1,0:T(8,128)(2,1)} async-done(((bf16[2,128,128]{2,1,0:T(8,128)(2,1)}), bf16[32,128,128]{2,1,0:T(8,128)(2,1)}) %all-gather.2.cloned.1.call-update) | async-done | bytes 1048592 | tf_op jit(solution)/shard_map/all_gather | solution.py:68
  113.1 2.0 %convolution_convert_fusion.1 = bf16[20,128,128]{2,0,1:T(8,128)(2,1)S(1)} fusion(bf16[32,128,128]{2,1,0:T(8,128)(2,1)} %all-gather.2.cloned.1.call-done, s32[20]{0:T(128)S(1)} %fusion.26), kind=kOutput, calls=%fused_computation.2 | convolution fusion | flops 21299840 | bytes 1704016 | tf_op jit(solution)/shard_map/bj,jxy->bxy/dot_general | solution.py:69
  115.1 0.1 slice.9
  115.2 0.8 copy.69
  116.0 0.7 copy.70
  (3 shorter events, 0.1 us)
Async XLA Ops:
  7.2 51.0 %copy-start = (f32[1,1,2,128,128]{4,3,2,1,0:T(8,128)S(1)}, f32[1,1,2,128,128]{4,3,2,1,0:T(8,128)}, u32[]{:S(2)}) copy-start(f32[1,1,2,128,128]{4,3,2,1,0:T(8,128)} %param.16) | copy-start | bytes 393220
  7.2 2.4 %copy-start.2 = (bf16[1,12,128,128]{3,2,1,0:T(8,128)(2,1)S(1)}, bf16[1,12,128,128]{3,2,1,0:T(8,128)(2,1)}, u32[]{:S(2)}) copy-start(bf16[1,12,128,128]{3,2,1,0:T(8,128)(2,1)} %param.9) | copy-start | bytes 1179652
  7.2 13.7 %reduce-scatter.4.cloned.1.call-start = ((), (), s32[]{:S(2)}) async-start(), calls=%async_computation.3 | async-start | bytes 786432
  7.2 2.6 %copy-start.7 = (s32[20,1]{0,1:T(1,128)S(1)}, s32[20,1]{0,1:T(1,128)}, u32[]{:S(2)}) copy-start(s32[20,1]{0,1:T(1,128)} %param.11) | copy-start | bytes 244
  9.5 103.6 %all-gather.2.cloned.1.call-start = ((), (), s32[]{:S(2)}) async-start(), calls=%async_computation.2 | async-start | bytes 1114112 | tf_op jit(solution)/shard_map/all_gather | solution.py:68
  56.9 0.9 copy-start.3
  56.9 1.2 copy-start.1
  56.9 1.7 %copy-start.4 = (f32[1,1,2,128,128]{4,3,2,1,0:T(8,128)S(1)}, f32[1,1,2,128,128]{4,3,2,1,0:T(8,128)}, u32[]{:S(2)}) copy-start(f32[1,1,2,128,128]{4,3,2,1,0:T(8,128)} %param.12) | copy-start | bytes 393220
  57.8 1.6 %copy-start.5 = (f32[1,1,2,128,128]{4,3,2,1,0:T(8,128)S(1)}, f32[1,1,2,128,128]{4,3,2,1,0:T(8,128)}, u32[]{:S(2)}) copy-start(f32[1,1,2,128,128]{4,3,2,1,0:T(8,128)} %param.14) | copy-start | bytes 393220
  57.8 2.7 %copy-start.6 = (f32[1,1,2,128,128]{4,3,2,1,0:T(8,128)S(1)}, f32[1,1,2,128,128]{4,3,2,1,0:T(8,128)}, u32[]{:S(2)}) copy-start(f32[1,1,2,128,128]{4,3,2,1,0:T(8,128)} %param.13) | copy-start | bytes 393220
Sparse Core Ops, SparseCore 0:
  10.2 10.6 reduce-scatter.3
  59.5 53.5 all-gather.1
where the time goes:
time: 124 us
  waiting for transfers between devices  61.8 us (50%)
  blocking collectives  33.3 us (27%)
  between operations  14.2 us (11%)
  local copies, waits for them, and re-layouts  7.18 us (6%)
  matrix products  5.23 us (4%)
  other arithmetic  1.86 us (2%)
    all_gather x1, waiting for transfers between devices, on_device(): everyone = lax.all_gather(rounded, 'dp', axis=0, tiled=True)  50.9 us
    all_to_all x1, blocking collectives, on_device(): lax.all_to_all(outgoing, 'dp', split_axis=0, concat_axis=0, tiled=True)  33.3 us
    unnamed x3, waiting for transfers between devices  10.9 us
    unnamed x22, local copies, waits for them, and re-layouts  6.1 us
  transfers between devices with their start and end apart: 2, of which 2 were waited for; matrix products, arithmetic and copies ran while one was open for 3% of the time, Pallas kernels for 0%

commit v1 on v0

--- a/solution.py
+++ b/solution.py
@@ -65,7 +65,9 @@
         second[0, 0],
     )
     rounded = new_weights.astype(jnp.bfloat16)
-    everyone = lax.all_gather(rounded, "dp", axis=0, tiled=True)
+    spread = jnp.broadcast_to(rounded[None], (dp_count,) + rounded.shape)
+    everyone = lax.all_to_all(spread, "dp", split_axis=0, concat_axis=0, tiled=True)
+    everyone = everyone.reshape(slot_count, side, side)
     picked = jnp.einsum(
         "bj,jxy->bxy", one_hot, everyone, preferred_element_type=jnp.float32
     ).astype(jnp.bfloat16)

time: 124 us -> 99.1 us (0.80)
  waiting for transfers between devices: 61.8 us -> 31.8 us
  starting transfers between devices: 0.08 us -> 4.21 us
  local copies, waits for them, and re-layouts: 7.18 us -> 9.78 us
  matrix products: 5.23 us -> 3.69 us
    all_gather x1 -> x0, waiting for transfers between devices: 50.9 us -> none  [on_device(): everyone = lax.all_gather(rounded, 'dp', axis=0, tiled=True)]
    all_to_all x0 -> x1, waiting for transfers between devices: none -> 20.9 us  [on_device(): lax.all_to_all(spread, 'dp', split_axis=0, concat_axis=0, tiled=True)]
    all_to_all x0 -> x1, starting transfers between devices: none -> 4.18 us  [on_device(): lax.all_to_all(spread, 'dp', split_axis=0, concat_axis=0, tiled=True)]
    broadcast_in_dim x0 -> x1, local copies, waits for them, and re-layouts: none -> 1.8 us  [on_device(): spread = jnp.broadcast_to(rounded[None], (dp_count,) + rounded.shape)]
    dot_general x1, matrix products: 1.95 us -> 0.42 us  [on_device(): jnp.einsum('bj,jxy->bxy', one_hot, everyone, preferred_element_type=jnp.f...]
    unnamed x3 -> x2, waiting for transfers between devices: 10.9 us -> 10.9 us
where the time goes in v1:
time: 99.1 us; the launch traced here: 98.8 us
  blocking collectives  33.3 us (34%)
  waiting for transfers between devices  31.8 us (32%)
  between operations  14.2 us (14%)
  local copies, waits for them, and re-layouts  9.78 us (10%)
  starting transfers between devices  4.21 us (4%)
  matrix products  3.69 us (4%)
  other arithmetic  1.84 us (2%)
    all_to_all x1, blocking collectives, on_device(): lax.all_to_all(outgoing, 'dp', split_axis=0, concat_axis=0, tiled=True)  33.3 us
    all_to_all x1, waiting for transfers between devices, on_device(): lax.all_to_all(spread, 'dp', split_axis=0, concat_axis=0, tiled=True)  20.9 us
    unnamed x2, waiting for transfers between devices  10.9 us
    unnamed x22, local copies, waits for them, and re-layouts  6.1 us
    all_to_all x1, starting transfers between devices, on_device(): lax.all_to_all(spread, 'dp', split_axis=0, concat_axis=0, tiled=True)  4.18 us
  transfers between devices with their start and end apart: 2, of which 2 were waited for; matrix products, arithmetic and copies ran while one was open for 3% of the time, Pallas kernels for 0%

profile of v1, /device:TPU:0, one launch (start us, length us, event | category | flops | bytes accessed | tf_op | source)
XLA Modules:
  0.0 98.8 jit_solution(16059088734202444467)
XLA Ops:
  7.2 0.0 copy-start
  7.2 0.0 copy-start.2
  7.2 0.0 reduce-scatter.4.cloned.1.call-start
  7.2 0.0 copy-start.7
  7.2 2.2 %copy.87 = bf16[2,8,128,128]{3,1,2,0:T(8,128)(2,1)} copy(bf16[2,8,128,128]{3,2,1,0:T(8,128)(2,1)} %bitcast.77) | data formatting | bytes 1048576
  9.5 0.0 reduce-scatter.4.cloned.1.call-update
  9.5 0.0 copy-done.2
  9.5 0.3 copy.88
  9.8 0.0 copy-done.7
  9.8 0.2 convert_reduce_fusion.1
  10.0 10.9 %reduce-scatter.4.cloned.1.call-done = bf16[8,16384]{1,0:T(8,128)(2,1)} async-done(((bf16[16,16384]{1,0:T(8,128)(2,1)}), bf16[8,16384]{1,0:T(8,128)(2,1)}) %reduce-scatter.4.cloned.1.call-update) | async-done | bytes 262160
  20.9 1.0 copy.89
  21.9 0.2 copy.90
  22.1 0.6 convolution_convert_fusion
  22.7 1.0 copy.57
  23.6 33.3 %all_to_all.10 = bf16[16,2,128,128]{3,1,2,0:T(2,128)(2,1)S(1)} all-to-all(bf16[16,2,128,128]{3,1,2,0:T(2,128)(2,1)S(1)} %copy.57), channel_id=1, replica_groups=mesh['dp'=16,'mp'=2] {'dp'}, dimensions={0} | all-to-all | bytes 2097152 | tf_op jit(solution)/shard_map/all_to_all | solution.py:56
  56.9 0.0 copy-start.3
  56.9 0.0 copy-start.1
  56.9 0.0 copy-start.4
  56.9 0.1 convert_reduce_fusion
  57.0 0.8 copy-done.3
  57.8 0.3 fusion.15
  58.1 0.0 copy-done.1
  58.1 0.1 fusion.11
  58.2 0.0 copy-done
  58.2 0.4 multiply_reduce_fusion
  58.6 0.0 copy-done.4
  58.6 0.7 fusion.17
  59.3 0.1 copy.70
  59.4 1.8 %broadcast_in_dim.11 = bf16[16,2,128,128]{3,1,2,0:T(2,128)(2,1)} broadcast(bf16[2,128,128]{2,0,1:T(2,128)(2,1)S(1)} %copy.70), dimensions={1,2,3} | broadcast | bytes 1114112 | tf_op jit(solution)/shard_map/broadcast_in_dim | solution.py:68
  61.2 0.0 copy-start.5
  61.2 0.0 copy-start.6
  61.2 4.2 %all-to-all-start.1 = ((bf16[16,2,128,128]{3,1,2,0:T(2,128)(2,1)}), bf16[16,2,128,128]{3,1,2,0:T(2,128)(2,1)S(1)}, u32[]{:S(2)}, u32[]{:S(2)}) async-start(bf16[16,2,128,128]{3,1,2,0:T(2,128)(2,1)} %broadcast_in_dim.11), calls=%async_computation.1 | async-start | bytes 2097152 | tf_op jit(solution)/shard_map/all_to_all | solution.py:69
  65.4 0.0 copy-done.5
  65.4 1.0 %fusion.1 = f32[1,1,2,128,128]{4,3,2,1,0:T(8,128)} fusion(f32[2,128,128]{2,1,0:T(8,128)S(1)} %convert_reduce_fusion, f32[1,1,2,128,128]{4,3,2,1,0:T(8,128)S(1)} %copy-done.5), kind=kOutput, calls=%fused_computation.5 | convolution fusion | flops 50429952 | bytes 393216 | tf_op jit(solution)/shard_map/...ji,...jk->...ik/dot_general | solution.py:28
  66.5 0.0 copy-done.6
  66.5 1.0 %fusion.3 = f32[1,1,2,128,128]{4,3,2,1,0:T(8,128)} fusion(f32[2,128,128]{2,1,0:T(8,128)S(1)} %convert_reduce_fusion, f32[1,1,2,128,128]{4,3,2,1,0:T(8,128)S(1)} %copy-done.6), kind=kOutput, calls=%fused_computation.8 | convolution fusion | flops 50429952 | bytes 393216 | tf_op jit(solution)/shard_map/...ij,...kj->...ik/dot_general | solution.py:25
  67.5 0.7 fusion.12
  68.2 20.9 %all-to-all-done.1 = bf16[16,2,128,128]{3,1,2,0:T(2,128)(2,1)S(1)} async-done(((bf16[16,2,128,128]{3,1,2,0:T(2,128)(2,1)}), bf16[16,2,128,128]{3,1,2,0:T(2,128)(2,1)S(1)}, u32[]{:S(2)}, u32[]{:S(2)}) %all-to-all-start.1) | async-done | bytes 1048608 | tf_op jit(solution)/shard_map/all_to_all | solution.py:69
  89.1 0.7 copy.71
  89.8 0.4 convolution_convert_fusion.1
  90.3 0.1 slice.9
  90.4 0.8 copy.72
  91.2 0.7 copy.73
  (3 shorter events, 0.1 us)
Async XLA Ops:
  7.2 51.0 %copy-start = (f32[1,1,2,128,128]{4,3,2,1,0:T(8,128)S(1)}, f32[1,1,2,128,128]{4,3,2,1,0:T(8,128)}, u32[]{:S(2)}) copy-start(f32[1,1,2,128,128]{4,3,2,1,0:T(8,128)} %param.16) | copy-start | bytes 393220
  7.2 2.3 %copy-start.2 = (bf16[1,12,128,128]{3,2,1,0:T(8,128)(2,1)S(1)}, bf16[1,12,128,128]{3,2,1,0:T(8,128)(2,1)}, u32[]{:S(2)}) copy-start(bf16[1,12,128,128]{3,2,1,0:T(8,128)(2,1)} %param.9) | copy-start | bytes 1179652
  7.2 13.7 %reduce-scatter.4.cloned.1.call-start = ((), (), s32[]{:S(2)}) async-start(), calls=%async_computation.3 | async-start | bytes 786432
  7.2 2.6 %copy-start.7 = (s32[20,1]{0,1:T(1,128)S(1)}, s32[20,1]{0,1:T(1,128)}, u32[]{:S(2)}) copy-start(s32[20,1]{0,1:T(1,128)} %param.11) | copy-start | bytes 244
  56.9 0.9 copy-start.3
  56.9 1.2 %copy-start.1 = (f32[1,1,2,128,128]{4,3,2,1,0:T(8,128)S(1)}, f32[1,1,2,128,128]{4,3,2,1,0:T(8,128)}, u32[]{:S(2)}) copy-start(f32[1,1,2,128,128]{4,3,2,1,0:T(8,128)} %param.17) | copy-start | bytes 393220
  56.9 1.7 %copy-start.4 = (f32[1,1,2,128,128]{4,3,2,1,0:T(8,128)S(1)}, f32[1,1,2,128,128]{4,3,2,1,0:T(8,128)}, u32[]{:S(2)}) copy-start(f32[1,1,2,128,128]{4,3,2,1,0:T(8,128)} %param.12) | copy-start | bytes 393220
  61.2 4.2 %copy-start.5 = (f32[1,1,2,128,128]{4,3,2,1,0:T(8,128)S(1)}, f32[1,1,2,128,128]{4,3,2,1,0:T(8,128)}, u32[]{:S(2)}) copy-start(f32[1,1,2,128,128]{4,3,2,1,0:T(8,128)} %param.14) | copy-start | bytes 393220
  61.2 5.2 %copy-start.6 = (f32[1,1,2,128,128]{4,3,2,1,0:T(8,128)S(1)}, f32[1,1,2,128,128]{4,3,2,1,0:T(8,128)}, u32[]{:S(2)}) copy-start(f32[1,1,2,128,128]{4,3,2,1,0:T(8,128)} %param.13) | copy-start | bytes 393220
  61.2 27.9 %all-to-all-start.1 = ((bf16[16,2,128,128]{3,1,2,0:T(2,128)(2,1)}), bf16[16,2,128,128]{3,1,2,0:T(2,128)(2,1)S(1)}, u32[]{:S(2)}, u32[]{:S(2)}) async-start(bf16[16,2,128,128]{3,1,2,0:T(2,128)(2,1)} %broadcast_in_dim.11), calls=%async_computation.1 | async-start | bytes 2097152 | tf_op jit(solution)/shard_map/all_to_all | solution.py:69
Sparse Core Ops, SparseCore 0:
  10.2 10.6 reduce-scatter.3

commit v2 on v1

--- a/solution.py
+++ b/solution.py
@@ -45,10 +45,19 @@
     slot_count = dp_count * capacity
     value_count = value_grads.shape[1]
     side = value_grads.shape[2]
-    key_part = lax.psum_scatter(
-        key_grads.astype(jnp.float32).astype(jnp.bfloat16), "mp", scatter_dimension=2, tiled=True
-    ).astype(jnp.float32)
-    key_rows = key_part[0, 0].astype(jnp.bfloat16)
+    mp_count = lax.axis_size("mp")
+    key_share = key_grads.shape[2] // mp_count
+    shares = key_grads[0, 0].reshape(mp_count, key_share, side, side)
+    if mp_count == 2:
+        mp_index = lax.axis_index("mp")
+        mine = lax.dynamic_index_in_dim(shares, mp_index, axis=0, keepdims=False)
+        theirs = lax.dynamic_index_in_dim(shares, 1 - mp_index, axis=0, keepdims=False)
+        arrived = lax.ppermute(theirs, "mp", perm=[(0, 1), (1, 0)])
+        key_sum = mine.astype(jnp.float32) + arrived.astype(jnp.float32)
+    else:
+        arrived = lax.all_to_all(shares, "mp", split_axis=0, concat_axis=0, tiled=True)
+        key_sum = jnp.sum(arrived, axis=0, dtype=jnp.float32)
+    key_rows = key_sum.astype(jnp.bfloat16)
     one_hot = slot_onehot(owners[:, 0], capacity, slot_count)
     blocks = jnp.concatenate([value_grads[0], key_rows], axis=0)
     placed = jnp.einsum("bj,bxy->jxy", one_hot, blocks, preferred_element_type=jnp.float32)

time: 99.1 us -> 75.3 us (0.76)
  between operations: 14.2 us -> 0.79 us
  waiting for transfers between devices: 31.8 us -> 21.6 us
  local copies, waits for them, and re-layouts: 9.78 us -> 7.68 us
  blocking collectives: 33.3 us -> 34.6 us
    unnamed x2 -> x0, waiting for transfers between devices: 10.9 us -> none
    unnamed x22 -> x19, local copies, waits for them, and re-layouts: 6.1 us -> 2.72 us
    all_to_all x1, blocking collectives: 33.3 us -> 34.6 us  [on_device(): lax.all_to_all(outgoing, 'dp', split_axis=0, concat_axis=0, tiled=True)]
    dynamic_slice x0 -> x2, local copies, waits for them, and re-layouts: none -> 1.3 us  [the longest x1 1.12 us: on_device(): mine = lax.dynamic_index_in_dim(shares, mp_index, axis=0, keepdims=False)]
  transfers between devices with their start and end apart: 2 -> 2, of which waited for: 2 -> 2; matrix products, arithmetic and copies ran while one was open for 3% -> 4% of each run, Pallas kernels for 0% -> 0%
where the time goes in v2:
time: 75.3 us; the launch traced here: 75 us
  blocking collectives  34.6 us (46%)
  waiting for transfers between devices  21.6 us (29%)
  local copies, waits for them, and re-layouts  7.68 us (10%)
  starting transfers between devices  4.64 us (6%)
  matrix products  3.7 us (5%)
  other arithmetic  2.01 us (3%)
  between operations  0.79 us (1%)
    all_to_all x1, blocking collectives, on_device(): lax.all_to_all(outgoing, 'dp', split_axis=0, concat_axis=0, tiled=True)  34.6 us
    all_to_all x1, waiting for transfers between devices, on_device(): lax.all_to_all(spread, 'dp', split_axis=0, concat_axis=0, tiled=True)  20.9 us
    all_to_all x1, starting transfers between devices, on_device(): lax.all_to_all(spread, 'dp', split_axis=0, concat_axis=0, tiled=True)  4.09 us
    unnamed x19, local copies, waits for them, and re-layouts  2.72 us
    broadcast_in_dim x1, local copies, waits for them, and re-layouts, on_device(): spread = jnp.broadcast_to(rounded[None], (dp_count,) + rounded.shape)  1.78 us
  transfers between devices with their start and end apart: 2, of which 2 were waited for; matrix products, arithmetic and copies ran while one was open for 4% of the time, Pallas kernels for 0%

profile of v2, /device:TPU:0, one launch (start us, length us, event | category | flops | bytes accessed | tf_op | source)
XLA Modules:
  0.0 75.0 jit_solution(4719605362160384894)
XLA Ops:
  0.6 0.0 copy-start
  0.6 0.0 copy-start.7
  0.7 0.0 copy-start.2
  0.7 1.1 %constant_dynamic-slice_fusion.1 = (bf16[1,8,128,128]{3,2,1,0:T(8,128)(2,1)S(1)}, bf16[1,8,128,128]{3,2,1,0:T(8,128)(2,1)S(1)}) fusion(bf16[2,8,128,128]{3,2,1,0:T(8,128)(2,1)} %bitcast.63, s32[]{:T(128)S(6)} %select_n.7, s32[]{:T(128)S(6)} %select_n.8), kind=kLoop, calls=%fused_computation.44 | loop fusion | bytes 1048584 | tf_op jit(solution)/shard_map/jit(dynamic_index_in_dim)/dynamic_slice | solution.py:53
  1.8 0.2 copy.96
  2.0 0.6 collective-permute-start
  2.5 0.0 copy-done.7
  2.5 0.2 convert_reduce_fusion.1
  2.7 0.0 copy-done.2
  2.7 0.3 copy.95
  3.0 0.7 collective-permute-done
  3.7 0.2 fusion.7
  3.9 0.6 convolution_convert_fusion
  4.4 1.0 %copy.68 = bf16[16,2,128,128]{3,1,2,0:T(2,128)(2,1)S(1)} copy(bf16[16,2,128,128]{3,1,0,2:T(2,128)(2,1)S(1)} %bitcast.60) | data formatting | bytes 2097152 | tf_op jit(solution)/shard_map/reshape | solution.py:64
  5.4 34.6 %all_to_all.10 = bf16[16,2,128,128]{3,1,2,0:T(2,128)(2,1)S(1)} all-to-all(bf16[16,2,128,128]{3,1,2,0:T(2,128)(2,1)S(1)} %copy.68), channel_id=1, replica_groups=mesh['dp'=16,'mp'=2] {'dp'}, dimensions={0} | all-to-all | bytes 2097152 | tf_op jit(solution)/shard_map/all_to_all | solution.py:65
  40.1 0.0 copy-start.3
  40.1 0.0 copy-start.1
  40.1 0.0 copy-start.4
  40.1 0.1 convert_reduce_fusion
  40.1 0.8 %copy-done.3 = f32[1,1,2,128,128]{4,3,2,1,0:T(8,128)S(1)} copy-done((f32[1,1,2,128,128]{4,3,2,1,0:T(8,128)S(1)}, f32[1,1,2,128,128]{4,3,2,1,0:T(8,128)}, u32[]{:S(2)}) %copy-start.3) | copy-done | bytes 131096
  41.0 0.3 fusion.16
  41.2 0.0 copy-done.1
  41.2 0.1 fusion.12
  41.4 0.0 copy-done
  41.4 0.4 multiply_reduce_fusion
  41.8 0.0 copy-done.4
  41.8 0.7 fusion.18
  42.5 0.1 copy.81
  42.6 1.8 %broadcast_in_dim.11 = bf16[16,2,128,128]{3,1,2,0:T(2,128)(2,1)} broadcast(bf16[2,128,128]{2,0,1:T(2,128)(2,1)S(1)} %copy.81), dimensions={1,2,3} | broadcast | bytes 1114112 | tf_op jit(solution)/shard_map/broadcast_in_dim | solution.py:77
  44.4 0.0 copy-start.5
  44.4 0.0 copy-start.6
  44.4 4.1 %all-to-all-start.1 = ((bf16[16,2,128,128]{3,1,2,0:T(2,128)(2,1)}), bf16[16,2,128,128]{3,1,2,0:T(2,128)(2,1)S(1)}, u32[]{:S(2)}, u32[]{:S(2)}) async-start(bf16[16,2,128,128]{3,1,2,0:T(2,128)(2,1)} %broadcast_in_dim.11), calls=%async_computation.1 | async-start | bytes 2097152 | tf_op jit(solution)/shard_map/all_to_all | solution.py:78
  48.5 0.0 copy-done.5
  48.5 1.0 %fusion.1 = f32[1,1,2,128,128]{4,3,2,1,0:T(8,128)} fusion(f32[2,128,128]{2,1,0:T(8,128)S(1)} %convert_reduce_fusion, f32[1,1,2,128,128]{4,3,2,1,0:T(8,128)S(1)} %copy-done.5), kind=kOutput, calls=%fused_computation.5 | convolution fusion | flops 50429952 | bytes 393216 | tf_op jit(solution)/shard_map/...ji,...jk->...ik/dot_general | solution.py:28
  49.5 0.0 copy-done.6
  49.5 1.0 %fusion.3 = f32[1,1,2,128,128]{4,3,2,1,0:T(8,128)} fusion(f32[2,128,128]{2,1,0:T(8,128)S(1)} %convert_reduce_fusion, f32[1,1,2,128,128]{4,3,2,1,0:T(8,128)S(1)} %copy-done.6), kind=kOutput, calls=%fused_computation.8 | convolution fusion | flops 50429952 | bytes 393216 | tf_op jit(solution)/shard_map/...ij,...kj->...ik/dot_general | solution.py:25
  50.6 0.7 fusion.13
  51.3 20.9 %all-to-all-done.1 = bf16[16,2,128,128]{3,1,2,0:T(2,128)(2,1)S(1)} async-done(((bf16[16,2,128,128]{3,1,2,0:T(2,128)(2,1)}), bf16[16,2,128,128]{3,1,2,0:T(2,128)(2,1)S(1)}, u32[]{:S(2)}, u32[]{:S(2)}) %all-to-all-start.1) | async-done | bytes 1048608 | tf_op jit(solution)/shard_map/all_to_all | solution.py:78
  72.1 0.7 copy.82
  72.9 0.4 convolution_convert_fusion.1
  73.3 0.1 slice.9
  73.4 0.8 %copy.83 = bf16[12,128,128]{2,1,0:T(8,128)(2,1)} copy(bf16[12,128,128]{2,0,1:T(8,128)(2,1)S(1)} %slice.8) | data formatting | bytes 786432
  74.3 0.7 copy.84
  (3 shorter events, 0.1 us)
Async XLA Ops:
  0.6 40.7 %copy-start = (f32[1,1,2,128,128]{4,3,2,1,0:T(8,128)S(1)}, f32[1,1,2,128,128]{4,3,2,1,0:T(8,128)}, u32[]{:S(2)}) copy-start(f32[1,1,2,128,128]{4,3,2,1,0:T(8,128)} %param.16) | copy-start | bytes 393220
  0.6 1.9 %copy-start.7 = (s32[20,1]{0,1:T(1,128)S(1)}, s32[20,1]{0,1:T(1,128)}, u32[]{:S(2)}) copy-start(s32[20,1]{0,1:T(1,128)} %param.11) | copy-start | bytes 244
  0.7 2.1 %copy-start.2 = (bf16[1,12,128,128]{3,2,1,0:T(8,128)(2,1)S(1)}, bf16[1,12,128,128]{3,2,1,0:T(8,128)(2,1)}, u32[]{:S(2)}) copy-start(bf16[1,12,128,128]{3,2,1,0:T(8,128)(2,1)} %param.9) | copy-start | bytes 1179652
  2.0 1.7 %collective-permute-start = (bf16[8,128,128]{2,0,1:T(8,128)(2,1)S(1)}, bf16[8,128,128]{2,0,1:T(8,128)(2,1)S(1)}, u32[]{:S(2)}, u32[]{:S(2)}) collective-permute-start(bf16[8,128,128]{2,0,1:T(8,128)(2,1)S(1)} %bitcast.64), channel_id=1, source_target_pairs={{0,1},{1,0},{2,3},{3,2},{4,5},{5,4},{6,7},{7,6},{8,9},{9,8},{10,11... | collective-permute-start | bytes 786440 | tf_op jit(solution)/shard_map/ppermute | solution.py:55
  40.1 0.9 %copy-start.3 = (f32[1,1,2,128,128]{4,3,2,1,0:T(8,128)S(1)}, f32[1,1,2,128,128]{4,3,2,1,0:T(8,128)}, u32[]{:S(2)}) copy-start(f32[1,1,2,128,128]{4,3,2,1,0:T(8,128)} %param.15) | copy-start | bytes 393220
  40.1 1.2 %copy-start.1 = (f32[1,1,2,128,128]{4,3,2,1,0:T(8,128)S(1)}, f32[1,1,2,128,128]{4,3,2,1,0:T(8,128)}, u32[]{:S(2)}) copy-start(f32[1,1,2,128,128]{4,3,2,1,0:T(8,128)} %param.17) | copy-start | bytes 393220
  40.1 1.7 %copy-start.4 = (f32[1,1,2,128,128]{4,3,2,1,0:T(8,128)S(1)}, f32[1,1,2,128,128]{4,3,2,1,0:T(8,128)}, u32[]{:S(2)}) copy-start(f32[1,1,2,128,128]{4,3,2,1,0:T(8,128)} %param.12) | copy-start | bytes 393220
  44.4 4.1 %copy-start.5 = (f32[1,1,2,128,128]{4,3,2,1,0:T(8,128)S(1)}, f32[1,1,2,128,128]{4,3,2,1,0:T(8,128)}, u32[]{:S(2)}) copy-start(f32[1,1,2,128,128]{4,3,2,1,0:T(8,128)} %param.14) | copy-start | bytes 393220
  44.4 5.2 %copy-start.6 = (f32[1,1,2,128,128]{4,3,2,1,0:T(8,128)S(1)}, f32[1,1,2,128,128]{4,3,2,1,0:T(8,128)}, u32[]{:S(2)}) copy-start(f32[1,1,2,128,128]{4,3,2,1,0:T(8,128)} %param.13) | copy-start | bytes 393220
  44.4 27.8 %all-to-all-start.1 = ((bf16[16,2,128,128]{3,1,2,0:T(2,128)(2,1)}), bf16[16,2,128,128]{3,1,2,0:T(2,128)(2,1)S(1)}, u32[]{:S(2)}, u32[]{:S(2)}) async-start(bf16[16,2,128,128]{3,1,2,0:T(2,128)(2,1)} %broadcast_in_dim.11), calls=%async_computation.1 | async-start | bytes 2097152 | tf_op jit(solution)/shard_map/all_to_all | solution.py:78
